TPU v7x, 32 devices: a whole 2x2x4 slice. The times are simulated.
32 devices in a mesh: groups: 2 (over y), ctx: 4 (over z), heads: 4 (over x, core).
Axes of the slice: x: 2, y: 2, z: 4, core: 2. Of those that a mesh axis runs over, the one named last changes fastest.
Arguments:
- queries: bfloat16 [2048, 4096], P(('groups', 'ctx'), 'heads'), parts along dimension 0
- keys: bfloat16 [2048, 1024], P(('groups', 'ctx'), 'heads'), parts along dimension 0
- values: bfloat16 [2048, 1024], P(('groups', 'ctx'), 'heads'), parts along dimension 0, may hold values from -6 to 6
- conv_kernel: float32 [32, 6, 11], P('heads')
- head_mix: float32 [8, 4, 4], P('heads')
- norm_gain: float32 [4096], P('heads'), may hold values from 0.5 to 1.5
- bounds: int32 [4], P('groups'), parts along dimension 0, may hold values from 0 to 1024, as said below
Outputs:
- attended: bfloat16 [2048, 4096], P(('groups', 'ctx'), 'heads'), parts along dimension 0
There are 2 independent parts, one for each index of `groups`. A program takes and returns all parts, laid end to end along the dimension named above; an argument that names none is the same for every part. Nothing has to cross between parts.
Inputs may be any that keep to these rules, and one draw needn't show every extreme that they name: bounds[0] < bounds[1], and bounds[1] >= 512.
All inputs are finite; a program needn't handle non-finite values.
Results may differ from a plain program's by a relative error of at most 0.0045.
Values may be sent and summed in bfloat16 or wider, within the bound.
No kernel may reach another device: no remote copies, remote signals or barrier semaphores. Data moves between devices by JAX's collectives and lax.ppermute only.
A program may use at most 64 MiB of HBM per device.

v0:
```python
import jax
import jax.numpy as jnp
from jax import lax
from jax.sharding import PartitionSpec as P

NEG_FILL = -1e30
EPSILON = 1e-06


def from_behind(value, axis, steps):
    count = lax.axis_size(axis)
    leading, last = (max(0, -steps), min(count, count - steps))
    return lax.ppermute(value, axis, [(source, source + steps) for source in range(leading, last)])


def conv_scores(zeroed, kernel, out_rows, out_cols, q_edge, k_edge):
    summed = jnp.zeros(zeroed.shape[:2] + (out_rows, out_cols), jnp.float32)
    for tap_row in range(kernel.shape[2]):
        for tap_col in range(kernel.shape[3]):
            summed = (
                summed
                + kernel[:, :, tap_row, tap_col][:, :, None, None]
                * zeroed[
                    :,
                    :,
                    q_edge - tap_row : q_edge - tap_row + out_rows,
                    2 * k_edge - tap_col : 2 * k_edge - tap_col + out_cols,
                ]
            )
    return summed


def per_device(queries, keys, values, conv_kernel, head_mix, norm_gain, bounds):
    num_rows = queries.shape[0]
    kv_local = head_mix.shape[0]
    heads_per_group = head_mix.shape[1]
    head_width = keys.shape[1] // kv_local
    q_taps = conv_kernel.shape[1]
    k_taps = conv_kernel.shape[2]
    q_edge = q_taps - 1
    k_edge = k_taps // 2
    score_scale = head_width ** (-0.5)
    ctx_size = lax.axis_size("ctx")
    row_first = lax.axis_index("ctx") * num_rows
    start_row = bounds[0]
    end_row = bounds[1]
    prior_rows = from_behind(queries[num_rows - q_edge :], "ctx", 1)
    query_ext = jnp.concatenate([prior_rows, queries], 0).reshape(
        num_rows + q_edge, kv_local, heads_per_group, head_width
    )
    kernel = conv_kernel.reshape(kv_local, heads_per_group, q_taps, k_taps)
    seg_rows = query_ext.shape[0] - q_edge
    ext_pos = row_first - q_edge + jnp.arange(seg_rows + q_edge, dtype=jnp.int32)
    pos = row_first + jnp.arange(seg_rows, dtype=jnp.int32)
    live = (pos >= start_row) & (pos < end_row)
    segments = ((query_ext, ext_pos, pos, live),)

    def attend(carry_state, segment, key_block, value_block, key_first):
        seg_queries, row_ext_pos, row_pos, row_live = segment
        seg_rows = row_pos.shape[0]
        run_max, run_sum, run_acc = carry_state
        key_count = value_block.shape[0]
        raw_scores = (
            jnp.einsum("rgmd,kgd->gmrk", seg_queries, key_block, preferred_element_type=jnp.float32)
            * score_scale
        )
        key_ext_pos = key_first - k_edge + jnp.arange(key_count + 2 * k_edge, dtype=jnp.int32)
        zeroed = jnp.where(key_ext_pos[None, :] <= row_ext_pos[:, None], raw_scores, 0.0)
        mixed_scores = conv_scores(zeroed, kernel, seg_rows, key_count, q_edge, k_edge)
        key_pos = key_first + jnp.arange(key_count, dtype=jnp.int32)
        valid_mask = (key_pos[None, :] <= row_pos[:, None]) & row_live[:, None]
        block_max = jnp.max(jnp.where(valid_mask, mixed_scores, NEG_FILL), axis=-1)
        new_max = jnp.maximum(run_max, block_max)
        weights = jnp.where(valid_mask, jnp.exp(mixed_scores - new_max[..., None]), 0.0)
        factor = jnp.exp(run_max - new_max)
        new_sum = run_sum * factor + jnp.sum(weights, axis=-1)
        product = jnp.einsum(
            "gmrk,kgd->rgmd",
            weights.astype(jnp.bfloat16),
            value_block,
            preferred_element_type=jnp.float32,
        )
        new_acc = run_acc * jnp.transpose(factor, (2, 0, 1))[..., None] + product
        return (new_max, new_sum, new_acc)

    def guarded(carry_state, segment, key_block, value_block, key_first):
        return attend(carry_state, segment, key_block, value_block, key_first)

    def guarded_all(states, key_block, value_block, key_first):
        return tuple(
            (
                guarded(states[idx], segments[idx], key_block, value_block, key_first)
                for idx in range(len(segments))
            )
        )

    def fresh_state(segment):
        seg_rows = segment[2].shape[0]
        return (
            jnp.full((kv_local, heads_per_group, seg_rows), NEG_FILL, jnp.float32),
            jnp.zeros((kv_local, heads_per_group, seg_rows), jnp.float32),
            jnp.zeros((seg_rows, kv_local, heads_per_group, head_width), jnp.float32),
        )

    initial = tuple((fresh_state(segment) for segment in segments))
    boundary = jnp.concatenate([keys[:k_edge], keys[num_rows - k_edge :]], 0)
    edge_table = lax.all_gather(boundary, "ctx", axis=0, tiled=True)
    edge_table = edge_table.reshape(ctx_size, 2 * k_edge, kv_local * head_width)
    blank_rows = jnp.zeros((1, 2 * k_edge, kv_local * head_width), keys.dtype)
    padded_table = jnp.concatenate([blank_rows, edge_table, blank_rows], 0)
    key_piece = lax.all_gather(keys, "ctx", axis=0, tiled=True)
    value_piece = lax.all_gather(values, "ctx", axis=0, tiled=True)
    shards = key_piece.shape[0] // num_rows
    key_split = key_piece.reshape(shards, num_rows, kv_local, head_width)
    value_split = value_piece.reshape(shards, num_rows, kv_local, head_width)

    def per_shard(shard_pos, inner_state):
        lower_edge = lax.dynamic_index_in_dim(padded_table, shard_pos, 0, keepdims=False)[k_edge:]
        upper_edge = lax.dynamic_index_in_dim(padded_table, shard_pos + 2, 0, keepdims=False)[
            :k_edge
        ]
        middle_keys = lax.dynamic_index_in_dim(key_split, shard_pos, 0, keepdims=False)
        block_keys = jnp.concatenate(
            [
                lower_edge.reshape(k_edge, kv_local, head_width),
                middle_keys,
                upper_edge.reshape(k_edge, kv_local, head_width),
            ],
            0,
        )
        block_values = lax.dynamic_index_in_dim(value_split, shard_pos, 0, keepdims=False)
        return guarded_all(inner_state, block_keys, block_values, shard_pos * num_rows)

    final_states = lax.fori_loop(0, shards, per_shard, initial)
    run_max, run_sum, run_acc = final_states[0]
    row_live = segments[0][3]
    seg_rows = row_live.shape[0]
    divisor = jnp.where(row_live[None, None, :], run_sum, 1.0)
    probs_out = run_acc / jnp.transpose(divisor, (2, 0, 1))[..., None]
    blended = jnp.einsum("gab,rgbd->rgad", head_mix, probs_out, precision=lax.Precision.HIGHEST)
    mean_sq = jnp.mean(blended * blended, axis=-1, keepdims=True)
    normed = (
        blended
        * lax.rsqrt(mean_sq + EPSILON)
        * norm_gain.reshape(kv_local, heads_per_group, head_width)
    )
    result = jnp.where(row_live[:, None, None, None], normed, 0.0)
    return result.reshape(seg_rows, kv_local * heads_per_group * head_width).astype(jnp.bfloat16)


def solution(mesh):
    return jax.shard_map(
        per_device,
        mesh=mesh,
        in_specs=(
            P(("groups", "ctx"), "heads"),
            P(("groups", "ctx"), "heads"),
            P(("groups", "ctx"), "heads"),
            P("heads", None, None),
            P("heads", None, None),
            P("heads"),
            P("groups"),
        ),
        out_specs=P(("groups", "ctx"), "heads"),
        check_vma=False,
    )
```

profile of v0, /device:TPU:0, one launch (start us, length us, event | category | flops | bytes accessed | tf_op | source)
XLA Modules:
  0.0 266.3 jit_solution(12256957341839974469)
XLA Ops:
  0.0 0.8 slice.1361
  0.8 4.9 %collective-permute-start = (bf16[5,1024]{1,0:T(8,128)(2,1)S(1)}, bf16[5,1024]{1,0:T(8,128)(2,1)S(1)}, u32[]{:S(2)}, u32[]{:S(2)}) collective-permute-start(bf16[5,1024]{1,0:T(8,128)(2,1)S(1)} %slice.1361), channel_id=1, source_target_pairs={{0,4},{4,8},{8,12},{1,5},{5,9},{9,13},{2,6},{6,10},{10,14},{3,7},{... | collective-permute-start | bytes 30728 | tf_op jit(solution)/shard_map/ppermute | solution.py:13
  5.8 0.7 fusion.89
  6.5 16.0 %all_gather.10 = bf16[1024,256]{1,0:T(8,128)(2,1)S(1)} all-gather(bf16[256,256]{1,0:T(8,128)(2,1)} %param.10), channel_id=1, replica_groups=mesh['groups'=2,'ctx'=4,'heads'=4] {'ctx'}, dimensions={0}, use_global_device_ids=true | all-gather | bytes 655360 | tf_op jit(solution)/shard_map/all_gather | solution.py:111
  22.4 13.1 %all-gather = bf16[4,10,256]{2,1,0:T(8,128)(2,1)S(1)} all-gather(bf16[1,10,256]{2,1,0:T(8,128)(2,1)S(1)} %maximum_bitcast_fusion.2), channel_id=1, replica_groups=mesh['groups'=2,'ctx'=4,'heads'=4] {'ctx'}, dimensions={0}, use_global_device_ids=true | all-gather | bytes 25600 | tf_op jit(solution)/shard_map/all_gather | solution.py:107
  35.6 1.3 fusion.90
  36.9 14.9 %all_gather.11 = bf16[1024,256]{1,0:T(8,128)(2,1)S(1)} all-gather(bf16[256,256]{1,0:T(8,128)(2,1)} %param.11), channel_id=1, replica_groups=mesh['groups'=2,'ctx'=4,'heads'=4] {'ctx'}, dimensions={0}, use_global_device_ids=true | all-gather | bytes 655360 | tf_op jit(solution)/shard_map/all_gather | solution.py:112
  51.8 1.7 compare_and_fusion.2
  53.6 0.9 reshape.80
  54.5 0.9 reshape.82
  55.7 0.3 reshape.81
  56.0 0.9 copy.34
  56.9 201.9 %while.22 = (s32[]{:T(128)}, f32[2,4,256]{2,1,0:T(4,128)S(1)}, f32[2,4,256]{2,1,0:T(4,128)S(1)}, f32[256,2,4,128]{0,3,2,1:T(8,128)}, f32[2,4,6,11]{1,0,3,2:T(2,1...) while((s32[]{:T(128)}, f32[2,4,256]{2,1,0:T(4,128)S(1)}, ...), condition=%wide.region_3.4_spmd.clone.clone.clone, body=%wide.region_0.3_spmd.clone.clone.clone.sunk | while | flops 351798912 | bytes 160064880 | solution.py:134
  56.9 1.2 constant_dynamic-slice_fusion.3
  58.0 0.7 copy.51
  58.9 1.9 bitcast_select_fusion.2
  60.7 1.2 compare_and_fusion.5
  62.1 0.7 slice_bitcast_fusion.70
  62.8 0.7 slice_bitcast_fusion.71
  63.4 0.7 slice_bitcast_fusion.72
  64.1 0.6 slice_bitcast_fusion.73
  64.7 38.1 %select_reduce_fusion.2 = (f32[2,4,256]{2,1,0:T(4,128)S(1)}, f32[2,4,256,256]{3,2,1,0:T(8,128)}) fusion(pred[256,256]{1,0:T(8,128)(4,1)S(1)} %compare_and_fusion.6, f32[2,4,261,266]{3,2,1,0:T(8,128)S(1)} %bitcast_select_fusion.2, f32[2,4]{1,0:T(2,128)S(1)} %get-tuple-element.735, f32[2,4]{1,0:T(2,128)S(1)} %get-tuple-element.736, ...), kind=kLoop, calls=%fused_computation.136.clone.1 | loop fusion | flops 69728256 | bytes 140585024 | tf_op jit(solution)/shard_map/while/body/eval_jaxpr/reduce_max | solution.py:72
  103.0 3.3 %fusion.106 = f32[256,2,4,128]{0,3,2,1:T(8,128)} fusion(f32[2,4,256,256]{3,2,1,0:T(8,128)} %get-tuple-element.803, f32[256,2,4,128]{0,3,2,1:T(8,128)} %get-tuple-element.829, f32[2,4,256]{2,1,0:T(4,128)S(1)} %get-tuple-element.847, pred[256,256]{1,0:T(8,128)(4,1)S(1)} %compare_and_fusion.6, f32[256,2,4]{0,2,1:T(4,128)S(1)} %get-tuple-element.804, ...), kind=kOutput, calls=%fused_computation.140.clone.1 | convolution fusion | flops 136577024 | bytes 4407297 | tf_op jit(solution)/shard_map/while/body/eval_jaxpr/gmrk,kgd->rgmd/dot_general | solution.py:77
  106.3 0.7 fusion.104
  107.2 1.2 constant_dynamic-slice_fusion.3
  108.3 0.7 copy.51
  109.2 1.9 bitcast_select_fusion.2
  111.0 1.2 compare_and_fusion.5
  112.4 0.7 slice_bitcast_fusion.70
  113.1 0.7 slice_bitcast_fusion.71
  113.7 0.7 slice_bitcast_fusion.72
  114.4 0.6 slice_bitcast_fusion.73
  115.0 38.1 %select_reduce_fusion.2 = (f32[2,4,256]{2,1,0:T(4,128)S(1)}, f32[2,4,256,256]{3,2,1,0:T(8,128)}) fusion(pred[256,256]{1,0:T(8,128)(4,1)S(1)} %compare_and_fusion.6, f32[2,4,261,266]{3,2,1,0:T(8,128)S(1)} %bitcast_select_fusion.2, f32[2,4]{1,0:T(2,128)S(1)} %get-tuple-element.735, f32[2,4]{1,0:T(2,128)S(1)} %get-tuple-element.736, ...), kind=kLoop, calls=%fused_computation.136.clone.1 | loop fusion | flops 69728256 | bytes 140585024 | tf_op jit(solution)/shard_map/while/body/eval_jaxpr/reduce_max | solution.py:72
  153.3 3.6 %fusion.106 = f32[256,2,4,128]{0,3,2,1:T(8,128)} fusion(f32[2,4,256,256]{3,2,1,0:T(8,128)} %get-tuple-element.803, f32[256,2,4,128]{0,3,2,1:T(8,128)} %get-tuple-element.829, f32[2,4,256]{2,1,0:T(4,128)S(1)} %get-tuple-element.847, pred[256,256]{1,0:T(8,128)(4,1)S(1)} %compare_and_fusion.6, f32[256,2,4]{0,2,1:T(4,128)S(1)} %get-tuple-element.804, ...), kind=kOutput, calls=%fused_computation.140.clone.1 | convolution fusion | flops 136577024 | bytes 4407297 | tf_op jit(solution)/shard_map/while/body/eval_jaxpr/gmrk,kgd->rgmd/dot_general | solution.py:77
  156.9 0.7 fusion.104
  157.7 1.2 constant_dynamic-slice_fusion.3
  158.9 0.7 copy.51
  159.7 1.9 bitcast_select_fusion.2
  161.6 1.2 compare_and_fusion.5
  163.0 0.7 slice_bitcast_fusion.70
  163.6 0.7 slice_bitcast_fusion.71
  164.3 0.7 slice_bitcast_fusion.72
  165.0 0.6 slice_bitcast_fusion.73
  165.6 38.1 %select_reduce_fusion.2 = (f32[2,4,256]{2,1,0:T(4,128)S(1)}, f32[2,4,256,256]{3,2,1,0:T(8,128)}) fusion(pred[256,256]{1,0:T(8,128)(4,1)S(1)} %compare_and_fusion.6, f32[2,4,261,266]{3,2,1,0:T(8,128)S(1)} %bitcast_select_fusion.2, f32[2,4]{1,0:T(2,128)S(1)} %get-tuple-element.735, f32[2,4]{1,0:T(2,128)S(1)} %get-tuple-element.736, ...), kind=kLoop, calls=%fused_computation.136.clone.1 | loop fusion | flops 69728256 | bytes 140585024 | tf_op jit(solution)/shard_map/while/body/eval_jaxpr/reduce_max | solution.py:72
  203.8 3.6 %fusion.106 = f32[256,2,4,128]{0,3,2,1:T(8,128)} fusion(f32[2,4,256,256]{3,2,1,0:T(8,128)} %get-tuple-element.803, f32[256,2,4,128]{0,3,2,1:T(8,128)} %get-tuple-element.829, f32[2,4,256]{2,1,0:T(4,128)S(1)} %get-tuple-element.847, pred[256,256]{1,0:T(8,128)(4,1)S(1)} %compare_and_fusion.6, f32[256,2,4]{0,2,1:T(4,128)S(1)} %get-tuple-element.804, ...), kind=kOutput, calls=%fused_computation.140.clone.1 | convolution fusion | flops 136577024 | bytes 4407297 | tf_op jit(solution)/shard_map/while/body/eval_jaxpr/gmrk,kgd->rgmd/dot_general | solution.py:77
  207.4 0.7 fusion.104
  208.3 1.2 constant_dynamic-slice_fusion.3
  209.5 0.7 copy.51
  210.3 1.9 bitcast_select_fusion.2
  212.1 1.2 compare_and_fusion.5
  213.5 0.7 slice_bitcast_fusion.70
  214.2 0.7 slice_bitcast_fusion.71
  214.9 0.7 slice_bitcast_fusion.72
  215.5 0.6 slice_bitcast_fusion.73
  216.1 38.1 %select_reduce_fusion.2 = (f32[2,4,256]{2,1,0:T(4,128)S(1)}, f32[2,4,256,256]{3,2,1,0:T(8,128)}) fusion(pred[256,256]{1,0:T(8,128)(4,1)S(1)} %compare_and_fusion.6, f32[2,4,261,266]{3,2,1,0:T(8,128)S(1)} %bitcast_select_fusion.2, f32[2,4]{1,0:T(2,128)S(1)} %get-tuple-element.735, f32[2,4]{1,0:T(2,128)S(1)} %get-tuple-element.736, ...), kind=kLoop, calls=%fused_computation.136.clone.1 | loop fusion | flops 69728256 | bytes 140585024 | tf_op jit(solution)/shard_map/while/body/eval_jaxpr/reduce_max | solution.py:72
  254.4 3.6 %fusion.106 = f32[256,2,4,128]{0,3,2,1:T(8,128)} fusion(f32[2,4,256,256]{3,2,1,0:T(8,128)} %get-tuple-element.803, f32[256,2,4,128]{0,3,2,1:T(8,128)} %get-tuple-element.829, f32[2,4,256]{2,1,0:T(4,128)S(1)} %get-tuple-element.847, pred[256,256]{1,0:T(8,128)(4,1)S(1)} %compare_and_fusion.6, f32[256,2,4]{0,2,1:T(4,128)S(1)} %get-tuple-element.804, ...), kind=kOutput, calls=%fused_computation.140.clone.1 | convolution fusion | flops 136577024 | bytes 4407297 | tf_op jit(solution)/shard_map/while/body/eval_jaxpr/gmrk,kgd->rgmd/dot_general | solution.py:77
  258.0 0.7 fusion.104
  258.8 0.6 select_bitcast_fusion
  259.4 1.3 broadcast_divide_fusion
  260.7 0.4 copy.36
  261.1 2.3 multiply_reduce_fusion
  263.5 1.5 select_convert_fusion
  265.0 0.3 copy.39
  265.3 1.0 copy.40
  (84 shorter events, 2.2 us)
Async XLA Ops:
  0.0 261.1 %copy-start = (f32[2,4,4]{2,1,0:T(4,128)S(1)}, f32[2,4,4]{2,1,0:T(4,128)}, u32[]{:S(2)}) copy-start(f32[2,4,4]{2,1,0:T(4,128)} %param.13) | copy-start | bytes 388
  0.0 55.5 %copy-start.2 = (bf16[256,1024]{1,0:T(8,128)(2,1)S(1)}, bf16[256,1024]{1,0:T(8,128)(2,1)}, u32[]{:S(2)}) copy-start(bf16[256,1024]{1,0:T(8,128)(2,1)} %param.9) | copy-start | bytes 1572868
  0.0 55.4 %copy-start.5 = (f32[8,6,11]{2,0,1:T(8,128)S(1)}, f32[8,6,11]{2,0,1:T(8,128)}, u32[]{:S(2)}) copy-start(f32[8,6,11]{2,0,1:T(8,128)} %param.12) | copy-start | bytes 6340
  0.8 54.7 %collective-permute-start = (bf16[5,1024]{1,0:T(8,128)(2,1)S(1)}, bf16[5,1024]{1,0:T(8,128)(2,1)S(1)}, u32[]{:S(2)}, u32[]{:S(2)}) collective-permute-start(bf16[5,1024]{1,0:T(8,128)(2,1)S(1)} %slice.1361), channel_id=1, source_target_pairs={{0,4},{4,8},{8,12},{1,5},{5,9},{9,13},{2,6},{6,10},{10,14},{3,7},{... | collective-permute-start | bytes 30728 | tf_op jit(solution)/shard_map/ppermute | solution.py:13
  56.9 2.0 copy-start.3
  103.0 3.4 %copy-start.1 = (f32[2,4,256,256]{3,2,1,0:T(8,128)S(1)}, f32[2,4,256,256]{3,2,1,0:T(8,128)}, u32[]{:S(2)}) copy-start(f32[2,4,256,256]{3,2,1,0:T(8,128)} %get-tuple-element.803) | copy-start | bytes 6291460 | tf_op jit(solution)/shard_map/while
  106.3 0.8 copy-start.4
  107.1 2.0 copy-start.3
  153.3 3.6 %copy-start.1 = (f32[2,4,256,256]{3,2,1,0:T(8,128)S(1)}, f32[2,4,256,256]{3,2,1,0:T(8,128)}, u32[]{:S(2)}) copy-start(f32[2,4,256,256]{3,2,1,0:T(8,128)} %get-tuple-element.803) | copy-start | bytes 6291460 | tf_op jit(solution)/shard_map/while
  156.9 0.8 copy-start.4
  157.7 2.0 copy-start.3
  203.8 3.6 %copy-start.1 = (f32[2,4,256,256]{3,2,1,0:T(8,128)S(1)}, f32[2,4,256,256]{3,2,1,0:T(8,128)}, u32[]{:S(2)}) copy-start(f32[2,4,256,256]{3,2,1,0:T(8,128)} %get-tuple-element.803) | copy-start | bytes 6291460 | tf_op jit(solution)/shard_map/while
  207.4 0.8 copy-start.4
  208.2 2.0 copy-start.3
  254.4 3.6 %copy-start.1 = (f32[2,4,256,256]{3,2,1,0:T(8,128)S(1)}, f32[2,4,256,256]{3,2,1,0:T(8,128)}, u32[]{:S(2)}) copy-start(f32[2,4,256,256]{3,2,1,0:T(8,128)} %get-tuple-element.803) | copy-start | bytes 6291460 | tf_op jit(solution)/shard_map/while
  258.0 0.8 copy-start.4
  260.7 2.8 %copy-start.6 = (pred[256]{0:T(512)(128)(4,1)S(1)}, pred[256]{0:T(512)(128)(4,1)}, u32[]{:S(2)}) copy-start(pred[256]{0:T(512)(128)(4,1)} %compare_and_fusion.2) | copy-start | bytes 772
  260.7 2.8 %copy-start.7 = (f32[1024]{0:T(1024)S(1)}, f32[1024]{0:T(1024)}, u32[]{:S(2)}) copy-start(f32[1024]{0:T(1024)} %param.14) | copy-start | bytes 12292
where the time goes:
time: 267 us; the launch traced here: 266 us
  other arithmetic  167 us (63%)
  blocking collectives  44 us (16%)
  local copies, waits for them, and re-layouts  26 us (10%)
  matrix products  23.9 us (9%)
  starting transfers between devices  4.95 us (2%)
    reduce_max x4, other arithmetic, attend(): block_max = jnp.max(jnp.where(valid_mask, mixed_scores, NEG_FILL), axis=-1)  152 us
    all_gather x1, blocking collectives, per_device(): key_piece = lax.all_gather(keys, 'ctx', axis=0, tiled=True)  16 us
    all_gather x1, blocking collectives, per_device(): value_piece = lax.all_gather(values, 'ctx', axis=0, tiled=True)  14.9 us
    dot_general x4, matrix products, attend(): jnp.einsum('gmrk,kgd->rgmd', weights.astype(jnp.bfloat16), value_block, p...  14.2 us
    all_gather x1, blocking collectives, per_device(): edge_table = lax.all_gather(boundary, 'ctx', axis=0, tiled=True)  13.1 us
    mul x16, local copies, waits for them, and re-layouts, conv_scores(): kernel[:, :, tap_row, tap_col][:, :, None, None]  10.4 us
    dot_general x4, matrix products, attend(): jnp.einsum('rgmd,kgd->gmrk', seg_queries, key_block, preferred_element_ty...  7.42 us
    and x5, other arithmetic, per_device(): live = (pos >= start_row) & (pos < end_row)  6.71 us
  transfers between devices with their start and end apart: 1, of which 0 were waited for; matrix products, arithmetic and copies ran while one was open for 2% of the time, Pallas kernels for 0%

commit v1 on v0

--- a/solution.py
+++ b/solution.py
@@ -109,7 +109,13 @@
     blank_rows = jnp.zeros((1, 2 * k_edge, kv_local * head_width), keys.dtype)
     padded_table = jnp.concatenate([blank_rows, edge_table, blank_rows], 0)
     key_piece = lax.all_gather(keys, "ctx", axis=0, tiled=True)
-    value_piece = lax.all_gather(values, "ctx", axis=0, tiled=True)
+    size = lax.axis_size("ctx")
+    held, tiles = (values, [values])
+    for _ in range(size - 1):
+        held = lax.ppermute(held, "ctx", [(i, (i + 1) % size) for i in range(size)])
+        tiles.insert(0, held)
+    line = jnp.concatenate(tiles, axis=0)
+    value_piece = jnp.roll(line, (lax.axis_index("ctx") + 1) * values.shape[0], axis=0)
     shards = key_piece.shape[0] // num_rows
     key_split = key_piece.reshape(shards, num_rows, kv_local, head_width)
     value_split = value_piece.reshape(shards, num_rows, kv_local, head_width)

time: 267 us -> 257 us (0.963)
  blocking collectives: 44 us -> 29.2 us
  starting transfers between devices: 4.95 us -> 8.27 us
    all_gather x1 -> x0, blocking collectives: 14.9 us -> none  [per_device(): value_piece = lax.all_gather(values, 'ctx', axis=0, tiled=True)]
    ppermute x0 -> x3, starting transfers between devices: none -> 4.8 us  [per_device(): held = lax.ppermute(held, 'ctx', [(i, (i + 1) % size) for i in range(size)])]
  transfers between devices with their start and end apart: 1 -> 4, of which waited for: 0 -> 1; matrix products, arithmetic and copies ran while one was open for 2% -> 3% of each run, Pallas kernels for 0% -> 0%
where the time goes in v1:
time: 257 us; the launch traced here: 256 us
  other arithmetic  167 us (65%)
  blocking collectives  29.2 us (11%)
  local copies, waits for them, and re-layouts  26.9 us (10%)
  matrix products  23.9 us (9%)
  starting transfers between devices  8.27 us (3%)
    reduce_max x4, other arithmetic, attend(): block_max = jnp.max(jnp.where(valid_mask, mixed_scores, NEG_FILL), axis=-1)  152 us
    all_gather x1, blocking collectives, per_device(): key_piece = lax.all_gather(keys, 'ctx', axis=0, tiled=True)  15.8 us
    dot_general x4, matrix products, attend(): jnp.einsum('gmrk,kgd->rgmd', weights.astype(jnp.bfloat16), value_block, p...  14.2 us
    all_gather x1, blocking collectives, per_device(): edge_table = lax.all_gather(boundary, 'ctx', axis=0, tiled=True)  13.5 us
    mul x16, local copies, waits for them, and re-layouts, conv_scores(): kernel[:, :, tap_row, tap_col][:, :, None, None]  10.4 us
    dot_general x4, matrix products, attend(): jnp.einsum('rgmd,kgd->gmrk', seg_queries, key_block, preferred_element_ty...  7.42 us
    and x5, other arithmetic, per_device(): live = (pos >= start_row) & (pos < end_row)  6.49 us
  transfers between devices with their start and end apart: 4, of which 1 were waited for; matrix products, arithmetic and copies ran while one was open for 3% of the time, Pallas kernels for 0%

profile of v1, /device:TPU:0, one launch (start us, length us, event | category | flops | bytes accessed | tf_op | source)
XLA Modules:
  0.0 255.9 jit_solution(3120452208323088006)
XLA Ops:
  0.0 3.1 %collective-permute-start.1 = (bf16[256,256]{1,0:T(8,128)(2,1)}, bf16[256,256]{1,0:T(8,128)(2,1)S(1)}, u32[]{:S(2)}, u32[]{:S(2)}) collective-permute-start(bf16[256,256]{1,0:T(8,128)(2,1)} %param.11), channel_id=1, source_target_pairs={{0,4},{4,8},{8,12},{12,0},{1,5},{5,9},{9,13},{13,1},{2,6},{6,10},{... | collective-permute-start | bytes 393224 | tf_op jit(solution)/shard_map/ppermute | solution.py:115
  3.1 0.7 slice.1361
  3.8 3.5 %collective-permute-start = (bf16[5,1024]{1,0:T(8,128)(2,1)S(1)}, bf16[5,1024]{1,0:T(8,128)(2,1)S(1)}, u32[]{:S(2)}, u32[]{:S(2)}) collective-permute-start(bf16[5,1024]{1,0:T(8,128)(2,1)S(1)} %slice.1361), channel_id=1, source_target_pairs={{0,4},{4,8},{8,12},{1,5},{5,9},{9,13},{2,6},{6,10},{10,14},{3,7},{... | collective-permute-start | bytes 30728 | tf_op jit(solution)/shard_map/ppermute | solution.py:13
  7.3 0.7 fusion.89
  8.0 15.8 %all_gather.7 = bf16[1024,256]{1,0:T(8,128)(2,1)S(1)} all-gather(bf16[256,256]{1,0:T(8,128)(2,1)} %param.10), channel_id=1, replica_groups=mesh['groups'=2,'ctx'=4,'heads'=4] {'ctx'}, dimensions={0}, use_global_device_ids=true | all-gather | bytes 655360 | tf_op jit(solution)/shard_map/all_gather | solution.py:111
  23.8 1.3 fusion.90
  25.1 13.5 %all-gather = bf16[4,10,256]{2,1,0:T(8,128)(2,1)S(1)} all-gather(bf16[1,10,256]{2,1,0:T(8,128)(2,1)S(1)} %maximum_bitcast_fusion.2), channel_id=1, replica_groups=mesh['groups'=2,'ctx'=4,'heads'=4] {'ctx'}, dimensions={0}, use_global_device_ids=true | all-gather | bytes 25600 | tf_op jit(solution)/shard_map/all_gather | solution.py:107
  38.6 1.7 collective-permute-start.3
  40.3 1.7 compare_and_fusion.2
  42.1 0.9 reshape.80
  43.0 0.9 copy.32
  44.4 0.9 copy.34
  45.7 0.9 reshape.82
  46.6 201.7 %while.22 = (s32[]{:T(128)}, f32[2,4,256]{2,1,0:T(4,128)S(1)}, f32[2,4,256]{2,1,0:T(4,128)S(1)}, f32[256,2,4,128]{0,3,2,1:T(8,128)}, f32[2,4,6,11]{1,0,3,2:T(2,1...) while((s32[]{:T(128)}, f32[2,4,256]{2,1,0:T(4,128)S(1)}, ...), condition=%wide.region_3.4_spmd.clone.clone.clone, body=%wide.region_0.3_spmd.clone.clone.clone.sunk | while | flops 351798912 | bytes 160064880 | solution.py:140
  46.6 1.2 constant_dynamic-slice_fusion.4
  47.8 0.7 copy.51
  48.6 1.9 bitcast_select_fusion.2
  50.5 1.2 compare_and_fusion.5
  51.8 0.7 slice_bitcast_fusion.70
  52.5 0.7 slice_bitcast_fusion.71
  53.1 0.7 slice_bitcast_fusion.72
  53.8 0.6 slice_bitcast_fusion.73
  54.4 38.1 %select_reduce_fusion.2 = (f32[2,4,256]{2,1,0:T(4,128)S(1)}, f32[2,4,256,256]{3,2,1,0:T(8,128)}) fusion(pred[256,256]{1,0:T(8,128)(4,1)S(1)} %compare_and_fusion.6, f32[2,4,261,266]{3,2,1,0:T(8,128)S(1)} %bitcast_select_fusion.2, f32[2,4]{1,0:T(2,128)S(1)} %get-tuple-element.735, f32[2,4]{1,0:T(2,128)S(1)} %get-tuple-element.736, ...), kind=kLoop, calls=%fused_computation.136.clone.1 | loop fusion | flops 69728256 | bytes 140585024 | tf_op jit(solution)/shard_map/while/body/eval_jaxpr/reduce_max | solution.py:72
  92.7 3.3 %fusion.106 = f32[256,2,4,128]{0,3,2,1:T(8,128)} fusion(f32[2,4,256,256]{3,2,1,0:T(8,128)} %get-tuple-element.803, f32[256,2,4,128]{0,3,2,1:T(8,128)} %get-tuple-element.829, f32[2,4,256]{2,1,0:T(4,128)S(1)} %get-tuple-element.847, pred[256,256]{1,0:T(8,128)(4,1)S(1)} %compare_and_fusion.6, f32[256,2,4]{0,2,1:T(4,128)S(1)} %get-tuple-element.804, ...), kind=kOutput, calls=%fused_computation.140.clone.1 | convolution fusion | flops 136577024 | bytes 4407297 | tf_op jit(solution)/shard_map/while/body/eval_jaxpr/gmrk,kgd->rgmd/dot_general | solution.py:77
  96.0 0.7 fusion.104
  96.9 1.2 constant_dynamic-slice_fusion.4
  98.0 0.7 copy.51
  98.9 1.9 bitcast_select_fusion.2
  100.7 1.2 compare_and_fusion.5
  102.1 0.7 slice_bitcast_fusion.70
  102.7 0.7 slice_bitcast_fusion.71
  103.4 0.7 slice_bitcast_fusion.72
  104.1 0.6 slice_bitcast_fusion.73
  104.7 38.1 %select_reduce_fusion.2 = (f32[2,4,256]{2,1,0:T(4,128)S(1)}, f32[2,4,256,256]{3,2,1,0:T(8,128)}) fusion(pred[256,256]{1,0:T(8,128)(4,1)S(1)} %compare_and_fusion.6, f32[2,4,261,266]{3,2,1,0:T(8,128)S(1)} %bitcast_select_fusion.2, f32[2,4]{1,0:T(2,128)S(1)} %get-tuple-element.735, f32[2,4]{1,0:T(2,128)S(1)} %get-tuple-element.736, ...), kind=kLoop, calls=%fused_computation.136.clone.1 | loop fusion | flops 69728256 | bytes 140585024 | tf_op jit(solution)/shard_map/while/body/eval_jaxpr/reduce_max | solution.py:72
  142.9 3.6 %fusion.106 = f32[256,2,4,128]{0,3,2,1:T(8,128)} fusion(f32[2,4,256,256]{3,2,1,0:T(8,128)} %get-tuple-element.803, f32[256,2,4,128]{0,3,2,1:T(8,128)} %get-tuple-element.829, f32[2,4,256]{2,1,0:T(4,128)S(1)} %get-tuple-element.847, pred[256,256]{1,0:T(8,128)(4,1)S(1)} %compare_and_fusion.6, f32[256,2,4]{0,2,1:T(4,128)S(1)} %get-tuple-element.804, ...), kind=kOutput, calls=%fused_computation.140.clone.1 | convolution fusion | flops 136577024 | bytes 4407297 | tf_op jit(solution)/shard_map/while/body/eval_jaxpr/gmrk,kgd->rgmd/dot_general | solution.py:77
  146.5 0.7 fusion.104
  147.4 1.2 constant_dynamic-slice_fusion.4
  148.5 0.7 copy.51
  149.4 1.9 bitcast_select_fusion.2
  151.2 1.2 compare_and_fusion.5
  152.6 0.7 slice_bitcast_fusion.70
  153.2 0.7 slice_bitcast_fusion.71
  153.9 0.7 slice_bitcast_fusion.72
  154.6 0.6 slice_bitcast_fusion.73
  155.2 38.1 %select_reduce_fusion.2 = (f32[2,4,256]{2,1,0:T(4,128)S(1)}, f32[2,4,256,256]{3,2,1,0:T(8,128)}) fusion(pred[256,256]{1,0:T(8,128)(4,1)S(1)} %compare_and_fusion.6, f32[2,4,261,266]{3,2,1,0:T(8,128)S(1)} %bitcast_select_fusion.2, f32[2,4]{1,0:T(2,128)S(1)} %get-tuple-element.735, f32[2,4]{1,0:T(2,128)S(1)} %get-tuple-element.736, ...), kind=kLoop, calls=%fused_computation.136.clone.1 | loop fusion | flops 69728256 | bytes 140585024 | tf_op jit(solution)/shard_map/while/body/eval_jaxpr/reduce_max | solution.py:72
  193.4 3.6 %fusion.106 = f32[256,2,4,128]{0,3,2,1:T(8,128)} fusion(f32[2,4,256,256]{3,2,1,0:T(8,128)} %get-tuple-element.803, f32[256,2,4,128]{0,3,2,1:T(8,128)} %get-tuple-element.829, f32[2,4,256]{2,1,0:T(4,128)S(1)} %get-tuple-element.847, pred[256,256]{1,0:T(8,128)(4,1)S(1)} %compare_and_fusion.6, f32[256,2,4]{0,2,1:T(4,128)S(1)} %get-tuple-element.804, ...), kind=kOutput, calls=%fused_computation.140.clone.1 | convolution fusion | flops 136577024 | bytes 4407297 | tf_op jit(solution)/shard_map/while/body/eval_jaxpr/gmrk,kgd->rgmd/dot_general | solution.py:77
  197.0 0.7 fusion.104
  197.9 1.2 constant_dynamic-slice_fusion.4
  199.0 0.7 copy.51
  199.9 1.9 bitcast_select_fusion.2
  201.7 1.2 compare_and_fusion.5
  203.1 0.7 slice_bitcast_fusion.70
  203.7 0.7 slice_bitcast_fusion.71
  204.4 0.7 slice_bitcast_fusion.72
  205.1 0.6 slice_bitcast_fusion.73
  205.7 38.1 %select_reduce_fusion.2 = (f32[2,4,256]{2,1,0:T(4,128)S(1)}, f32[2,4,256,256]{3,2,1,0:T(8,128)}) fusion(pred[256,256]{1,0:T(8,128)(4,1)S(1)} %compare_and_fusion.6, f32[2,4,261,266]{3,2,1,0:T(8,128)S(1)} %bitcast_select_fusion.2, f32[2,4]{1,0:T(2,128)S(1)} %get-tuple-element.735, f32[2,4]{1,0:T(2,128)S(1)} %get-tuple-element.736, ...), kind=kLoop, calls=%fused_computation.136.clone.1 | loop fusion | flops 69728256 | bytes 140585024 | tf_op jit(solution)/shard_map/while/body/eval_jaxpr/reduce_max | solution.py:72
  243.9 3.6 %fusion.106 = f32[256,2,4,128]{0,3,2,1:T(8,128)} fusion(f32[2,4,256,256]{3,2,1,0:T(8,128)} %get-tuple-element.803, f32[256,2,4,128]{0,3,2,1:T(8,128)} %get-tuple-element.829, f32[2,4,256]{2,1,0:T(4,128)S(1)} %get-tuple-element.847, pred[256,256]{1,0:T(8,128)(4,1)S(1)} %compare_and_fusion.6, f32[256,2,4]{0,2,1:T(4,128)S(1)} %get-tuple-element.804, ...), kind=kOutput, calls=%fused_computation.140.clone.1 | convolution fusion | flops 136577024 | bytes 4407297 | tf_op jit(solution)/shard_map/while/body/eval_jaxpr/gmrk,kgd->rgmd/dot_general | solution.py:77
  247.5 0.7 fusion.104
  248.3 0.7 select_bitcast_fusion
  249.0 1.3 broadcast_divide_fusion
  250.3 0.4 copy.36
  250.7 2.3 multiply_reduce_fusion
  253.1 1.5 select_convert_fusion
  254.9 1.0 copy.40
  (98 shorter events, 3.0 us)
Async XLA Ops:
  0.0 250.7 %copy-start = (f32[2,4,4]{2,1,0:T(4,128)S(1)}, f32[2,4,4]{2,1,0:T(4,128)}, u32[]{:S(2)}) copy-start(f32[2,4,4]{2,1,0:T(4,128)} %param.13) | copy-start | bytes 388
  0.0 43.9 %copy-start.2 = (bf16[256,1024]{1,0:T(8,128)(2,1)S(1)}, bf16[256,1024]{1,0:T(8,128)(2,1)}, u32[]{:S(2)}) copy-start(bf16[256,1024]{1,0:T(8,128)(2,1)} %param.9) | copy-start | bytes 1572868
  0.0 23.8 %collective-permute-start.1 = (bf16[256,256]{1,0:T(8,128)(2,1)}, bf16[256,256]{1,0:T(8,128)(2,1)S(1)}, u32[]{:S(2)}, u32[]{:S(2)}) collective-permute-start(bf16[256,256]{1,0:T(8,128)(2,1)} %param.11), channel_id=1, source_target_pairs={{0,4},{4,8},{8,12},{12,0},{1,5},{5,9},{9,13},{13,1},{2,6},{6,10},{... | collective-permute-start | bytes 393224 | tf_op jit(solution)/shard_map/ppermute | solution.py:115
  3.8 40.2 %collective-permute-start = (bf16[5,1024]{1,0:T(8,128)(2,1)S(1)}, bf16[5,1024]{1,0:T(8,128)(2,1)S(1)}, u32[]{:S(2)}, u32[]{:S(2)}) collective-permute-start(bf16[5,1024]{1,0:T(8,128)(2,1)S(1)} %slice.1361), channel_id=1, source_target_pairs={{0,4},{4,8},{8,12},{1,5},{5,9},{9,13},{2,6},{6,10},{10,14},{3,7},{... | collective-permute-start | bytes 30728 | tf_op jit(solution)/shard_map/ppermute | solution.py:13
  23.8 14.9 %collective-permute-start.2 = (bf16[256,256]{1,0:T(8,128)(2,1)S(1)}, bf16[256,256]{1,0:T(8,128)(2,1)S(1)}, u32[]{:S(2)}, u32[]{:S(2)}) collective-permute-start(bf16[256,256]{1,0:T(8,128)(2,1)S(1)} %collective-permute-done.1), channel_id=1, source_target_pairs={{0,4},{4,8},{8,12},{12,0},{1,5},{5,9},{9,13},{13,1},{2,6},{6,10},{... | collective-permute-start | bytes 393224 | tf_op jit(solution)/shard_map/ppermute | solution.py:115
  38.6 6.8 %collective-permute-start.3 = (bf16[256,256]{1,0:T(8,128)(2,1)S(1)}, bf16[256,256]{1,0:T(8,128)(2,1)S(1)}, u32[]{:S(2)}, u32[]{:S(2)}) collective-permute-start(bf16[256,256]{1,0:T(8,128)(2,1)S(1)} %collective-permute-done.2), channel_id=1, source_target_pairs={{0,4},{4,8},{8,12},{12,0},{1,5},{5,9},{9,13},{13,1},{2,6},{6,10},{... | collective-permute-start | bytes 393224 | tf_op jit(solution)/shard_map/ppermute | solution.py:115
  43.0 2.5 copy-start.3
  46.6 2.0 copy-start.4
  92.7 3.4 %copy-start.1 = (f32[2,4,256,256]{3,2,1,0:T(8,128)S(1)}, f32[2,4,256,256]{3,2,1,0:T(8,128)}, u32[]{:S(2)}) copy-start(f32[2,4,256,256]{3,2,1,0:T(8,128)} %get-tuple-element.803) | copy-start | bytes 6291460 | tf_op jit(solution)/shard_map/while
  96.0 0.8 copy-start.5
  96.8 2.0 copy-start.4
  142.9 3.6 %copy-start.1 = (f32[2,4,256,256]{3,2,1,0:T(8,128)S(1)}, f32[2,4,256,256]{3,2,1,0:T(8,128)}, u32[]{:S(2)}) copy-start(f32[2,4,256,256]{3,2,1,0:T(8,128)} %get-tuple-element.803) | copy-start | bytes 6291460 | tf_op jit(solution)/shard_map/while
  146.5 0.8 copy-start.5
  147.3 2.0 copy-start.4
  193.4 3.6 %copy-start.1 = (f32[2,4,256,256]{3,2,1,0:T(8,128)S(1)}, f32[2,4,256,256]{3,2,1,0:T(8,128)}, u32[]{:S(2)}) copy-start(f32[2,4,256,256]{3,2,1,0:T(8,128)} %get-tuple-element.803) | copy-start | bytes 6291460 | tf_op jit(solution)/shard_map/while
  197.0 0.8 copy-start.5
  197.8 2.0 copy-start.4
  243.9 3.6 %copy-start.1 = (f32[2,4,256,256]{3,2,1,0:T(8,128)S(1)}, f32[2,4,256,256]{3,2,1,0:T(8,128)}, u32[]{:S(2)}) copy-start(f32[2,4,256,256]{3,2,1,0:T(8,128)} %get-tuple-element.803) | copy-start | bytes 6291460 | tf_op jit(solution)/shard_map/while
  247.5 0.8 copy-start.5
  250.3 2.8 %copy-start.6 = (pred[256]{0:T(512)(128)(4,1)S(1)}, pred[256]{0:T(512)(128)(4,1)}, u32[]{:S(2)}) copy-start(pred[256]{0:T(512)(128)(4,1)} %compare_and_fusion.2) | copy-start | bytes 772
  250.3 2.8 %copy-start.7 = (f32[1024]{0:T(1024)S(1)}, f32[1024]{0:T(1024)}, u32[]{:S(2)}) copy-start(f32[1024]{0:T(1024)} %param.14) | copy-start | bytes 12292
